TPU v7x, 32 devices: a whole 2x2x4 slice. The times are simulated.
32 devices in a mesh: section: 4 (over z), dp: 4 (over y, x), tensor: 2 (over core).
Axes of the slice: x: 2, y: 2, z: 4, core: 2. Of those that a mesh axis runs over, the one named last changes fastest.
Arguments:
- sent_out: bfloat16 [4, 2, 768, 4096], P('section', None, 'dp', 'tensor'), may hold values from -6 to 6
- sent_back: bfloat16 [4, 2, 768, 4096], P('section', None, 'dp', 'tensor'), may hold values from -6 to 6
- sent_grad: bfloat16 [4, 2, 768, 4096], P('section', None, 'dp', 'tensor'), may hold values from -6 to 6
- lengths: int32 [4, 4], P('section', 'dp'), may hold values from 48 to 192
- weight: bfloat16 [4, 4096, 4096], P('section', 'dp', 'tensor'), may hold values from -0.09375 to 0.09375
Outputs:
- emitted: bfloat16 [4, 2, 768, 4096], P('section', None, 'dp', 'tensor')
- rebuilt: bfloat16 [4, 2, 768, 4096], P('section', None, 'dp', 'tensor')
- input_grad: bfloat16 [4, 2, 768, 4096], P('section', None, 'dp', 'tensor')
- weight_grad: bfloat16 [4, 4096, 4096], P('section', 'dp', 'tensor')
All inputs are finite; a program needn't handle non-finite values.
Results may differ from a plain program's by a relative error of at most 0.0075.
Values may be sent and summed in bfloat16 or wider, within the bound.
A program may use at most 128 MiB of HBM per device.

v0:
```python
import jax
import jax.numpy as jnp
from jax import lax
from jax.sharding import PartitionSpec as P


def shifted(block, axis, distance):
    devices = range(lax.axis_size(axis))
    route = [((i - distance) % len(devices), i) for i in devices]
    return lax.ppermute(block, axis, route)


def across_rows(left, right):
    return lax.dot_general(
        left, right, (((0,), (0,)), ((), ())), preferred_element_type=jnp.float32
    )


def slope(hidden):
    sigma = jax.nn.sigmoid(hidden)
    return sigma * (1.0 + hidden * (1.0 - sigma))


def local(sent_out, sent_back, sent_grad, lengths, weight):
    token_rows = sent_out.shape[2]
    local_weight = weight[0]
    whole_weight = lax.all_gather(local_weight, "dp", axis=0, tiled=True)
    inbound = shifted(sent_out, "section", 1)
    upper_in = inbound[0, 0]
    lower_in = inbound[0, 1]
    upper_full = lax.all_gather(upper_in, "tensor", axis=1, tiled=True)
    pre = jnp.dot(upper_full, whole_weight, preferred_element_type=jnp.float32)
    upper_out = (lower_in.astype(jnp.float32) + jax.nn.silu(pre)).astype(jnp.bfloat16)
    emitted = jnp.stack([upper_out, upper_in])[None]
    back, incoming = shifted((sent_back, sent_grad), "section", -1)
    back_upper = back[0, 0]
    back_lower = back[0, 1]
    lower_full = lax.all_gather(back_lower, "tensor", axis=1, tiled=True)
    pre_held = jnp.dot(lower_full, whole_weight, preferred_element_type=jnp.float32)
    rebuilt_lower = (back_upper.astype(jnp.float32) - jax.nn.silu(pre_held)).astype(jnp.bfloat16)
    rebuilt = jnp.stack([back_lower, rebuilt_lower])[None]
    keep = (jnp.arange(token_rows, dtype=jnp.int32) < lengths[0, 0])[:, None]
    zero = jnp.zeros((), jnp.bfloat16)
    dupper = jnp.where(keep, incoming[0, 0], zero)
    dlower = jnp.where(keep, incoming[0, 1], zero)
    hidden = (dupper.astype(jnp.float32) * slope(pre_held)).astype(jnp.bfloat16)
    terms = lax.dot_general(
        hidden, whole_weight, (((1,), (1,)), ((), ())), preferred_element_type=jnp.float32
    )
    through = lax.psum_scatter(
        terms.astype(jnp.bfloat16), "tensor", scatter_dimension=1, tiled=True
    ).astype(jnp.float32)
    dupper_in = (dlower.astype(jnp.float32) + through).astype(jnp.bfloat16)
    grads_out = jnp.stack([dupper_in, dupper])[None]
    held_share = lax.all_to_all(lower_full, "dp", split_axis=1, concat_axis=0, tiled=True)
    hidden_all = lax.all_gather(hidden, "dp", axis=0, tiled=True)
    weight_grad = across_rows(held_share, hidden_all).astype(jnp.bfloat16)[None]
    rebuilt, grads_out, weight_grad = (rebuilt, grads_out, weight_grad)
    return (emitted, rebuilt, grads_out, weight_grad)


def solution(mesh):
    return jax.shard_map(
        local,
        mesh=mesh,
        in_specs=(
            P("section", None, "dp", "tensor"),
            P("section", None, "dp", "tensor"),
            P("section", None, "dp", "tensor"),
            P("section", "dp"),
            P("section", "dp", "tensor"),
        ),
        out_specs=(
            P("section", None, "dp", "tensor"),
            P("section", None, "dp", "tensor"),
            P("section", None, "dp", "tensor"),
            P("section", "dp", "tensor"),
        ),
        check_vma=False,
    )
```

profile of v0, /device:TPU:0, one launch (start us, length us, event | category | flops | bytes accessed | tf_op | source)
XLA Modules:
  0.0 327.9 jit_solution(17365934528555776995)
XLA Ops:
  7.2 5.1 %collective-permute-start.1 = (bf16[1,2,192,2048]{3,2,1,0:T(8,128)(2,1)}, bf16[1,2,192,2048]{3,2,1,0:T(8,128)(2,1)S(1)}, u32[]{:S(2)}, u32[]{:S(2)}) collective-permute-start(bf16[1,2,192,2048]{3,2,1,0:T(8,128)(2,1)} %param.6), channel_id=1, source_target_pairs={{8,0},{16,8},{24,16},{0,24},{9,1},{17,9},{25,17},{1,25},{10,2},{18... | collective-permute-start | bytes 4718600 | tf_op jit(solution)/shard_map/ppermute | solution.py:10
  12.3 34.0 %collective-permute-done.1 = bf16[1,2,192,2048]{3,2,1,0:T(8,128)(2,1)S(1)} collective-permute-done((bf16[1,2,192,2048]{3,2,1,0:T(8,128)(2,1)}, bf16[1,2,192,2048]{3,2,1,0:T(8,128)(2,1)S(1)}, u32[]{:S(2)}, u32[]{:S(2)}) %collective-permute-start.1) | collective-permute-done | bytes 1572896 | tf_op jit(solution)/shard_map/ppermute | solution.py:10
  46.3 1.1 copy-done.5
  47.5 1.1 slice_bitcast_fusion.3
  48.5 0.0 all-gather.12.cloned.1.call-start
  48.6 0.7 all-gather.12.cloned.1.call-update
  49.3 0.4 collective-permute-start
  49.7 3.9 %collective-permute-start.2 = (bf16[1,2,192,2048]{3,2,1,0:T(8,128)(2,1)}, bf16[1,2,192,2048]{3,2,1,0:T(8,128)(2,1)S(1)}, u32[]{:S(2)}, u32[]{:S(2)}) collective-permute-start(bf16[1,2,192,2048]{3,2,1,0:T(8,128)(2,1)} %param.7), channel_id=1, source_target_pairs={{8,0},{16,8},{24,16},{0,24},{9,1},{17,9},{25,17},{1,25},{10,2},{18... | collective-permute-start | bytes 4718600 | tf_op jit(solution)/shard_map/ppermute | solution.py:10
  54.3 34.9 %collective-permute-done = bf16[1,2,192,2048]{3,2,1,0:T(8,128)(2,1)} collective-permute-done((bf16[1,2,192,2048]{3,2,1,0:T(8,128)(2,1)}, bf16[1,2,192,2048]{3,2,1,0:T(8,128)(2,1)}, u32[]{:S(2)}, u32[]{:S(2)}) %collective-permute-start) | collective-permute-done | bytes 1572896 | tf_op jit(solution)/shard_map/ppermute | solution.py:10
  89.2 2.5 fusion.17
  91.7 0.0 reduce-scatter.2.cloned.1.call-start
  91.7 26.9 %collective-permute-done.2 = bf16[1,2,192,2048]{3,2,1,0:T(8,128)(2,1)S(1)} collective-permute-done((bf16[1,2,192,2048]{3,2,1,0:T(8,128)(2,1)}, bf16[1,2,192,2048]{3,2,1,0:T(8,128)(2,1)S(1)}, u32[]{:S(2)}, u32[]{:S(2)}) %collective-permute-start.2) | collective-permute-done | bytes 1572896 | tf_op jit(solution)/shard_map/ppermute | solution.py:10
  118.7 102.0 %all-gather.12.cloned.1.call-done = bf16[1,4096,2048]{2,1,0:T(8,128)(2,1)} async-done(((bf16[1,1024,2048]{2,1,0:T(8,128)(2,1)}), bf16[1,4096,2048]{2,1,0:T(8,128)(2,1)}) %all-gather.12.cloned.1.call-update) | async-done | bytes 16777232 | tf_op jit(solution)/shard_map/all_gather | solution.py:27
  220.7 11.4 %multiply_convert_fusion = (bf16[192,2048]{1,0:T(8,128)(2,1)S(1)}, bf16[1,192,2048]{2,1,0:T(8,128)(2,1)}) fusion(pred[192]{0:T(512)(128)(4,1)S(1)} %iota_compare_fusion, bf16[1,2,192,2048]{3,2,1,0:T(8,128)(2,1)S(1)} %collective-permute-done.2, bf16[1,2,192,2048]{3,2,1,0:T(8,128)(2,1)} %copy-done.5, ...), kind=kOutput, calls=%fused_computation.18 | convolution fusion | flops 3227123712 | bytes 21496000 | tf_op jit(solution)/shard_map/dot_general | solution.py:39
  232.0 12.8 %fusion.6 = bf16[192,4096]{1,0:T(8,128)(2,1)} fusion(bf16[192,2048]{1,0:T(8,128)(2,1)S(1)} %get-tuple-element.12, bf16[1,4096,2048]{2,1,0:T(8,128)(2,1)} %all-gather.12.cloned.1.call-done), kind=kOutput, calls=%fused_computation.6 | convolution fusion | flops 3222011904 | bytes 19136512 | tf_op jit(solution)/shard_map/dot_general | solution.py:47
  244.9 0.0 all-gather.8.cloned.1.call-start
  244.9 0.5 all-gather.8.cloned.1.call-update
  245.5 0.1 bitcast_select_fusion
  245.6 2.9 all_to_all.14
  248.5 1.7 copy.10
  250.2 4.5 %all-to-all-start = ((bf16[192,4,1024]{2,0,1:T(8,128)(2,1)}), bf16[192,4,1024]{2,0,1:T(8,128)(2,1)}, u32[]{:S(2)}, u32[]{:S(2)}) async-start(bf16[192,4,1024]{2,0,1:T(8,128)(2,1)} %copy.10), calls=%async_computation.1 | async-start | bytes 3145728 | tf_op jit(solution)/shard_map/all_to_all | solution.py:55
  254.8 10.0 %fusion.15 = bf16[1,192,2048]{2,1,0:T(8,128)(2,1)S(1)} fusion(bf16[1,2,192,2048]{3,2,1,0:T(8,128)(2,1)} %collective-permute-done, bf16[1,4096,2048]{2,1,0:T(8,128)(2,1)} %all-gather.12.cloned.1.call-done, bf16[1,1,192,4096]{3,2,1,0:T(8,128)(2,1)} %all-gather.10.cloned.1.call-done), kind=kOutput, calls=%fused_computation.27 | convolution fusion | flops 3223977984 | bytes 19922944 | tf_op jit(solution)/shard_map/dot_general | solution.py:32
  264.9 1.3 maximum_bitcast_fusion
  266.1 0.1 copy-done.4
  266.2 1.3 maximum_bitcast_fusion.1
  267.5 0.7 copy-done.2
  268.2 1.4 fusion.13
  269.6 1.3 maximum_bitcast_fusion.2
  270.9 11.0 %all-to-all-done = bf16[192,4,1024]{2,0,1:T(8,128)(2,1)} async-done(((bf16[192,4,1024]{2,0,1:T(8,128)(2,1)}), bf16[192,4,1024]{2,0,1:T(8,128)(2,1)}, u32[]{:S(2)}, u32[]{:S(2)}) %all-to-all-start) | async-done | bytes 1572896 | tf_op jit(solution)/shard_map/all_to_all | solution.py:55
  281.9 25.3 %all-gather.8.cloned.1.call-done = bf16[768,2048]{1,0:T(8,128)(2,1)} async-done(((bf16[192,2048]{1,0:T(8,128)(2,1)}), bf16[768,2048]{1,0:T(8,128)(2,1)}) %all-gather.8.cloned.1.call-update) | async-done | bytes 3145744 | tf_op jit(solution)/shard_map/all_gather | solution.py:56
  307.2 7.8 %convert_bitcast_fusion = bf16[1,1024,2048]{1,2,0:T(8,128)(2,1)} fusion(bf16[768,2048]{1,0:T(8,128)(2,1)} %all-gather.8.cloned.1.call-done, bf16[768,1024]{1,0:T(8,128)(2,1)} %bitcast.18), kind=kOutput, calls=%fused_computation.7 | convolution fusion | flops 3223322624 | bytes 8912896 | tf_op jit(solution)/shard_map/dot_general | solution.py:14
  314.9 6.4 %copy.11 = bf16[1,1024,2048]{2,1,0:T(8,128)(2,1)} copy(bf16[1,1024,2048]{1,2,0:T(8,128)(2,1)} %convert_bitcast_fusion) | data formatting | bytes 8388608
  (18 shorter events, 0.2 us)
Async XLA Ops:
  7.2 111.5 %all-gather.14.cloned.1.call-start = ((), (), s32[]{:S(2)}) async-start(), calls=%async_computation.6 | async-start | bytes 2359296 | tf_op jit(solution)/shard_map/all_gather | solution.py:38
  7.2 39.1 %collective-permute-start.1 = (bf16[1,2,192,2048]{3,2,1,0:T(8,128)(2,1)}, bf16[1,2,192,2048]{3,2,1,0:T(8,128)(2,1)S(1)}, u32[]{:S(2)}, u32[]{:S(2)}) collective-permute-start(bf16[1,2,192,2048]{3,2,1,0:T(8,128)(2,1)} %param.6), channel_id=1, source_target_pairs={{8,0},{16,8},{24,16},{0,24},{9,1},{17,9},{25,17},{1,25},{10,2},{18... | collective-permute-start | bytes 4718600 | tf_op jit(solution)/shard_map/ppermute | solution.py:10
  46.3 1.1 copy-start.5
  48.5 172.1 %all-gather.12.cloned.1.call-start = ((), (), s32[]{:S(2)}) async-start(), calls=%async_computation.5 | async-start | bytes 20971520 | tf_op jit(solution)/shard_map/all_gather | solution.py:27
  49.3 205.5 %all-gather.10.cloned.1.call-start = ((), (), s32[]{:S(2)}) async-start(), calls=%async_computation.4 | async-start | bytes 2359296 | tf_op jit(solution)/shard_map/all_gather | solution.py:31
  49.3 39.8 %collective-permute-start = (bf16[1,2,192,2048]{3,2,1,0:T(8,128)(2,1)}, bf16[1,2,192,2048]{3,2,1,0:T(8,128)(2,1)}, u32[]{:S(2)}, u32[]{:S(2)}) collective-permute-start(bf16[1,2,192,2048]{3,2,1,0:T(8,128)(2,1)} %param.5), channel_id=1, source_target_pairs={{24,0},{0,8},{8,16},{16,24},{25,1},{1,9},{9,17},{17,25},{26,2},{2,... | collective-permute-start | bytes 4718600 | tf_op jit(solution)/shard_map/ppermute | solution.py:10
  49.7 68.9 %collective-permute-start.2 = (bf16[1,2,192,2048]{3,2,1,0:T(8,128)(2,1)}, bf16[1,2,192,2048]{3,2,1,0:T(8,128)(2,1)S(1)}, u32[]{:S(2)}, u32[]{:S(2)}) collective-permute-start(bf16[1,2,192,2048]{3,2,1,0:T(8,128)(2,1)} %param.7), channel_id=1, source_target_pairs={{8,0},{16,8},{24,16},{0,24},{9,1},{17,9},{25,17},{1,25},{10,2},{18... | collective-permute-start | bytes 4718600 | tf_op jit(solution)/shard_map/ppermute | solution.py:10
  91.7 175.8 %reduce-scatter.2.cloned.1.call-start = ((), (), s32[]{:S(2)}) async-start(), calls=%async_computation.2 | async-start | bytes 2359296 | tf_op jit(solution)/shard_map/reduce_scatter | solution.py:50
  118.7 126.8 %copy-start.1 = (bf16[1,2,192,2048]{3,2,1,0:T(8,128)(2,1)}, bf16[1,2,192,2048]{3,2,1,0:T(8,128)(2,1)S(1)}, u32[]{:S(2)}) copy-start(bf16[1,2,192,2048]{3,2,1,0:T(8,128)(2,1)S(1)} %collective-permute-done.2) | copy-start | bytes 4718596
  232.0 12.8 %copy-start.3 = (bf16[192,2048]{1,0:T(8,128)(2,1)}, bf16[192,2048]{1,0:T(8,128)(2,1)S(1)}, u32[]{:S(2)}) copy-start(bf16[192,2048]{1,0:T(8,128)(2,1)S(1)} %get-tuple-element.12) | copy-start | bytes 2359300
  244.9 62.3 %all-gather.8.cloned.1.call-start = ((), (), s32[]{:S(2)}) async-start(), calls=%async_computation.3 | async-start | bytes 3932160 | tf_op jit(solution)/shard_map/all_gather | solution.py:56
  250.2 31.6 %all-to-all-start = ((bf16[192,4,1024]{2,0,1:T(8,128)(2,1)}), bf16[192,4,1024]{2,0,1:T(8,128)(2,1)}, u32[]{:S(2)}, u32[]{:S(2)}) async-start(bf16[192,4,1024]{2,0,1:T(8,128)(2,1)} %copy.10), calls=%async_computation.1 | async-start | bytes 3145728 | tf_op jit(solution)/shard_map/all_to_all | solution.py:55
  254.8 10.0 %copy-start = (bf16[1,192,2048]{2,1,0:T(8,128)(2,1)S(1)}, bf16[1,192,2048]{2,1,0:T(8,128)(2,1)}, u32[]{:S(2)}) copy-start(bf16[1,192,2048]{2,1,0:T(8,128)(2,1)} %get-tuple-element.17) | copy-start | bytes 2359300
  264.8 1.4 copy-start.4
  266.2 2.0 copy-start.2
Sparse Core Ops, SparseCore 0:
  48.7 11.6 all-gather.13
  62.2 158.4 all-gather.11
  222.8 9.7 all-gather.9
  245.0 8.9 reduce-scatter.1
  255.7 51.4 all-gather.7
where the time goes:
time: 329 us; the launch traced here: 328 us
  waiting for transfers between devices  235 us (71%)
  matrix products  42 us (13%)
  local copies, waits for them, and re-layouts  16.5 us (5%)
  between operations  14.5 us (4%)
  starting transfers between devices  14.2 us (4%)
  other arithmetic  5.4 us (2%)
    all_gather x1, waiting for transfers between devices, local(): whole_weight = lax.all_gather(local_weight, 'dp', axis=0, tiled=True)  102 us
    ppermute x3, waiting for transfers between devices, shifted(): return lax.ppermute(block, axis, route)  95.8 us
    all_gather x1, waiting for transfers between devices, local(): hidden_all = lax.all_gather(hidden, 'dp', axis=0, tiled=True)  25.3 us
    dot_general x1, matrix products, local(): lax.dot_general(hidden, whole_weight, (((1,), (1,)), ((), ())), preferred...  12.8 us
    dot_general x1, matrix products, local(): jnp.dot(lower_full, whole_weight, preferred_element_type=jnp.float32)  11.4 us
    all_to_all x1, waiting for transfers between devices, local(): lax.all_to_all(lower_full, 'dp', split_axis=1, concat_axis=0, tiled=True)  11 us
    dot_general x1, matrix products, local(): pre = jnp.dot(upper_full, whole_weight, preferred_element_type=jnp.float32)  9.98 us
    ppermute x3, starting transfers between devices, shifted(): return lax.ppermute(block, axis, route)  9.43 us
  transfers between devices with their start and end apart: 9, of which 6 were waited for; matrix products, arithmetic and copies ran while one was open for 13% of the time, Pallas kernels for 0%

commit v1 on v0

--- a/solution.py
+++ b/solution.py
@@ -1,7 +1,24 @@
+import functools
 import jax
 import jax.numpy as jnp
 from jax import lax
 from jax.sharding import PartitionSpec as P
+
+
+def turn_signs(target, axis_name):
+    num_devices = lax.axis_size(axis_name)
+    buffers = [target]
+    for h in range(num_devices - 1):
+        placed = lax.ppermute(
+            buffers[-1], axis_name, [(p, (p + 1) % num_devices) for p in range(num_devices)]
+        )
+        buffers.append(placed)
+    found_now = jnp.concatenate(buffers[::-1], 0)
+    w_next = lax.axis_index(axis_name)
+    return jnp.roll(found_now, (w_next + 1) * target.shape[0], 0)
+
+
+recover_panels_by_axis = functools.partial(turn_signs, axis_name="dp")
 
 
 def shifted(block, axis, distance):
@@ -53,7 +70,7 @@
     dupper_in = (dlower.astype(jnp.float32) + through).astype(jnp.bfloat16)
     grads_out = jnp.stack([dupper_in, dupper])[None]
     held_share = lax.all_to_all(lower_full, "dp", split_axis=1, concat_axis=0, tiled=True)
-    hidden_all = lax.all_gather(hidden, "dp", axis=0, tiled=True)
+    hidden_all = recover_panels_by_axis(hidden)
     weight_grad = across_rows(held_share, hidden_all).astype(jnp.bfloat16)[None]
     rebuilt, grads_out, weight_grad = (rebuilt, grads_out, weight_grad)
     return (emitted, rebuilt, grads_out, weight_grad)

time: 329 us -> 337 us (1.024)
  local copies, waits for them, and re-layouts: 16.5 us -> 24.9 us
    ppermute x0 -> x3, waiting for transfers between devices: none -> 32.2 us  [turn_signs(): lax.ppermute(buffers[-1], axis_name, [(p, (p + 1) % num_devices) for p in...]
    all_gather x1, waiting for transfers between devices: 102 us -> 132 us  [local(): whole_weight = lax.all_gather(local_weight, 'dp', axis=0, tiled=True)]
    ppermute x3, waiting for transfers between devices: 95.8 us -> 68.1 us  [shifted(): return lax.ppermute(block, axis, route)]
    all_gather x1 -> x0, waiting for transfers between devices: 25.3 us -> none  [local(): hidden_all = lax.all_gather(hidden, 'dp', axis=0, tiled=True)]
    all_to_all x1, waiting for transfers between devices: 11 us -> 0.01 us  [local(): lax.all_to_all(lower_full, 'dp', split_axis=1, concat_axis=0, tiled=True)]
    unnamed x13 -> x24, local copies, waits for them, and re-layouts: 8.36 us -> 15.6 us
  transfers between devices with their start and end apart: 9 -> 11, of which waited for: 6 -> 6; matrix products, arithmetic and copies ran while one was open for 13% -> 19% of each run, Pallas kernels for 0% -> 0%
where the time goes in v1:
time: 337 us
  waiting for transfers between devices  233 us (69%)
  matrix products  41.8 us (12%)
  local copies, waits for them, and re-layouts  24.9 us (7%)
  starting transfers between devices  16.3 us (5%)
  between operations  14.5 us (4%)
  other arithmetic  6.37 us (2%)
    all_gather x1, waiting for transfers between devices, local(): whole_weight = lax.all_gather(local_weight, 'dp', axis=0, tiled=True)  132 us
    ppermute x3, waiting for transfers between devices, shifted(): return lax.ppermute(block, axis, route)  68.1 us
    ppermute x3, waiting for transfers between devices, turn_signs(): lax.ppermute(buffers[-1], axis_name, [(p, (p + 1) % num_devices) for p in...  32.2 us
    unnamed x24, local copies, waits for them, and re-layouts  15.6 us
    dot_general x1, matrix products, local(): lax.dot_general(hidden, whole_weight, (((1,), (1,)), ((), ())), preferred...  12.6 us
    dot_general x1, matrix products, local(): jnp.dot(lower_full, whole_weight, preferred_element_type=jnp.float32)  11.4 us
    dot_general x1, matrix products, local(): pre = jnp.dot(upper_full, whole_weight, preferred_element_type=jnp.float32)  9.98 us
    ppermute x3, starting transfers between devices, shifted(): return lax.ppermute(block, axis, route)  9.31 us
  transfers between devices with their start and end apart: 11, of which 6 were waited for; matrix products, arithmetic and copies ran while one was open for 19% of the time, Pallas kernels for 0%

profile of v1, /device:TPU:0, one launch (start us, length us, event | category | flops | bytes accessed | tf_op | source)
XLA Modules:
  0.0 336.7 jit_solution(4016009844788604710)
XLA Ops:
  7.2 5.1 %collective-permute-start.1 = (bf16[1,2,192,2048]{3,2,1,0:T(8,128)(2,1)}, bf16[1,2,192,2048]{3,2,1,0:T(8,128)(2,1)S(1)}, u32[]{:S(2)}, u32[]{:S(2)}) collective-permute-start(bf16[1,2,192,2048]{3,2,1,0:T(8,128)(2,1)} %param.6), channel_id=1, source_target_pairs={{8,0},{16,8},{24,16},{0,24},{9,1},{17,9},{25,17},{1,25},{10,2},{18... | collective-permute-start | bytes 4718600 | tf_op jit(solution)/shard_map/ppermute | solution.py:27
  12.3 34.0 %collective-permute-done.1 = bf16[1,2,192,2048]{3,2,1,0:T(8,128)(2,1)S(1)} collective-permute-done((bf16[1,2,192,2048]{3,2,1,0:T(8,128)(2,1)}, bf16[1,2,192,2048]{3,2,1,0:T(8,128)(2,1)S(1)}, u32[]{:S(2)}, u32[]{:S(2)}) %collective-permute-start.1) | collective-permute-done | bytes 1572896 | tf_op jit(solution)/shard_map/ppermute | solution.py:27
  46.3 1.1 copy-done.6
  47.5 1.4 slice_bitcast_fusion.3
  50.3 4.2 %collective-permute-start.2 = (bf16[1,2,192,2048]{3,2,1,0:T(8,128)(2,1)S(1)}, bf16[1,2,192,2048]{3,2,1,0:T(8,128)(2,1)S(1)}, u32[]{:S(2)}, u32[]{:S(2)}) collective-permute-start(bf16[1,2,192,2048]{3,2,1,0:T(8,128)(2,1)S(1)} %copy-done.7), channel_id=1, source_target_pairs={{8,0},{16,8},{24,16},{0,24},{9,1},{17,9},{25,17},{1,25},{10,2},{18... | collective-permute-start | bytes 4718600 | tf_op jit(solution)/shard_map/ppermute | solution.py:27
  55.1 34.1 %collective-permute-done.2 = bf16[1,2,192,2048]{3,2,1,0:T(8,128)(2,1)S(1)} collective-permute-done((bf16[1,2,192,2048]{3,2,1,0:T(8,128)(2,1)S(1)}, bf16[1,2,192,2048]{3,2,1,0:T(8,128)(2,1)S(1)}, u32[]{:S(2)}, u32[]{:S(2)}) %collective-permute-start.2) | collective-permute-done | bytes 1572896 | tf_op jit(solution)/shard_map/ppermute | solution.py:27
  89.2 131.7 %all-gather.9.cloned.1.call-done = bf16[1,4096,2048]{2,1,0:T(8,128)(2,1)} async-done(((bf16[1,1024,2048]{2,1,0:T(8,128)(2,1)}), bf16[1,4096,2048]{2,1,0:T(8,128)(2,1)}) %all-gather.9.cloned.1.call-update) | async-done | bytes 16777232 | tf_op jit(solution)/shard_map/all_gather | solution.py:44
  221.0 11.4 %multiply_convert_fusion = (bf16[192,2048]{1,0:T(8,128)(2,1)S(1)}, bf16[1,192,2048]{2,1,0:T(8,128)(2,1)}) fusion(pred[192]{0:T(512)(128)(4,1)S(1)} %iota_compare_fusion, bf16[1,2,192,2048]{3,2,1,0:T(8,128)(2,1)S(1)} %collective-permute-done.2, bf16[1,2,192,2048]{3,2,1,0:T(8,128)(2,1)} %copy-done.6, bf16[1,4096,2048]{2,1,0:T(8,128)(2,1)} %all-gather.9.cloned.1.call-done, ...), kind=kOutput, calls=%fused_computation.19 | convolution fusion | flops 3227123712 | bytes 21496000 | tf_op jit(solution)/shard_map/dot_general | solution.py:56
  232.3 1.5 collective-permute-start.3
  233.8 2.5 fusion.19
  236.3 1.0 bitcast_select_fusion
  237.3 2.9 all_to_all.14
  240.2 1.6 copy.10
  241.8 4.4 %all-to-all-start = ((bf16[192,4,1024]{2,0,1:T(8,128)(2,1)}), bf16[192,4,1024]{2,0,1:T(8,128)(2,1)}, u32[]{:S(2)}, u32[]{:S(2)}) async-start(bf16[192,4,1024]{2,0,1:T(8,128)(2,1)} %copy.10), calls=%async_computation.1 | async-start | bytes 3145728 | tf_op jit(solution)/shard_map/all_to_all | solution.py:72
  246.3 7.5 %collective-permute-done.3 = bf16[192,2048]{1,0:T(8,128)(2,1)S(1)} collective-permute-done((bf16[192,2048]{1,0:T(8,128)(2,1)S(1)}, bf16[192,2048]{1,0:T(8,128)(2,1)S(1)}, u32[]{:S(2)}, u32[]{:S(2)}) %collective-permute-start.3) | collective-permute-done | bytes 786464 | tf_op jit(solution)/shard_map/ppermute | solution.py:12
  254.2 12.6 %fusion.6 = bf16[192,4096]{1,0:T(8,128)(2,1)} fusion(bf16[192,2048]{1,0:T(8,128)(2,1)S(1)} %get-tuple-element.12, bf16[1,4096,2048]{2,1,0:T(8,128)(2,1)} %all-gather.9.cloned.1.call-done), kind=kOutput, calls=%fused_computation.6 | convolution fusion | flops 3222011904 | bytes 19136512 | tf_op jit(solution)/shard_map/dot_general | solution.py:64
  266.8 19.3 %collective-permute-done.4 = bf16[192,2048]{1,0:T(8,128)(2,1)S(1)} collective-permute-done((bf16[192,2048]{1,0:T(8,128)(2,1)S(1)}, bf16[192,2048]{1,0:T(8,128)(2,1)S(1)}, u32[]{:S(2)}, u32[]{:S(2)}) %collective-permute-start.4) | collective-permute-done | bytes 786464 | tf_op jit(solution)/shard_map/ppermute | solution.py:12
  286.6 10.0 %fusion.16 = bf16[1,192,2048]{2,1,0:T(8,128)(2,1)S(1)} fusion(bf16[1,2,192,2048]{3,2,1,0:T(8,128)(2,1)} %collective-permute-done, bf16[1,4096,2048]{2,1,0:T(8,128)(2,1)} %all-gather.9.cloned.1.call-done, bf16[1,1,192,4096]{3,2,1,0:T(8,128)(2,1)} %all-gather.7.cloned.1.call-done), kind=kOutput, calls=%fused_computation.28 | convolution fusion | flops 3223977984 | bytes 19922944 | tf_op jit(solution)/shard_map/dot_general | solution.py:49
  296.7 1.3 maximum_bitcast_fusion
  298.6 1.3 maximum_bitcast_fusion.1
  299.9 5.4 %collective-permute-done.5 = bf16[192,2048]{1,0:T(8,128)(2,1)S(1)} collective-permute-done((bf16[192,2048]{1,0:T(8,128)(2,1)S(1)}, bf16[192,2048]{1,0:T(8,128)(2,1)S(1)}, u32[]{:S(2)}, u32[]{:S(2)}) %collective-permute-start.5) | collective-permute-done | bytes 786464 | tf_op jit(solution)/shard_map/ppermute | solution.py:12
  305.3 0.9 constant_dynamic-update-slice_fusion.7
  306.2 1.0 constant_dynamic-update-slice_fusion.6
  307.2 1.0 constant_dynamic-update-slice_fusion.5
  308.2 0.9 constant_dynamic-update-slice_fusion.4
  310.0 0.9 constant_dynamic-update-slice_fusion.2
  311.0 1.0 constant_dynamic-update-slice_fusion.1
  312.0 0.9 constant_dynamic-update-slice_fusion
  312.9 7.9 %convert_bitcast_fusion = bf16[1,1024,2048]{1,2,0:T(8,128)(2,1)} fusion(bf16[768,1024]{1,0:T(8,128)(2,1)} %bitcast.18, bf16[1536,2048]{1,0:T(8,128)(2,1)} %constant_dynamic-update-slice_fusion, s32[]{:T(128)S(6)} %select_n.33), kind=kOutput, calls=%fused_computation.7 | convolution fusion | flops 3223322624 | bytes 8912900 | tf_op jit(solution)/shard_map/dot_general | solution.py:31
  320.8 6.5 %copy.11 = bf16[1,1024,2048]{2,1,0:T(8,128)(2,1)} copy(bf16[1,1024,2048]{1,2,0:T(8,128)(2,1)} %convert_bitcast_fusion) | data formatting | bytes 8388608
  327.4 1.5 fusion.14
  328.9 1.3 maximum_bitcast_fusion.2
  (33 shorter events, 4.1 us)
Async XLA Ops:
  7.2 82.1 %all-gather.11.cloned.1.call-start = ((), (), s32[]{:S(2)}) async-start(), calls=%async_computation.5 | async-start | bytes 2359296 | tf_op jit(solution)/shard_map/all_gather | solution.py:55
  7.2 39.1 %collective-permute-start.1 = (bf16[1,2,192,2048]{3,2,1,0:T(8,128)(2,1)}, bf16[1,2,192,2048]{3,2,1,0:T(8,128)(2,1)S(1)}, u32[]{:S(2)}, u32[]{:S(2)}) collective-permute-start(bf16[1,2,192,2048]{3,2,1,0:T(8,128)(2,1)} %param.6), channel_id=1, source_target_pairs={{8,0},{16,8},{24,16},{0,24},{9,1},{17,9},{25,17},{1,25},{10,2},{18... | collective-permute-start | bytes 4718600 | tf_op jit(solution)/shard_map/ppermute | solution.py:27
  46.3 1.1 copy-start.6
  48.9 1.4 copy-start.7
  48.9 172.1 %all-gather.9.cloned.1.call-start = ((), (), s32[]{:S(2)}) async-start(), calls=%async_computation.4 | async-start | bytes 20971520 | tf_op jit(solution)/shard_map/all_gather | solution.py:44
  49.6 237.0 %all-gather.7.cloned.1.call-start = ((), (), s32[]{:S(2)}) async-start(), calls=%async_computation.3 | async-start | bytes 2359296 | tf_op jit(solution)/shard_map/all_gather | solution.py:48
  50.3 39.0 %collective-permute-start.2 = (bf16[1,2,192,2048]{3,2,1,0:T(8,128)(2,1)S(1)}, bf16[1,2,192,2048]{3,2,1,0:T(8,128)(2,1)S(1)}, u32[]{:S(2)}, u32[]{:S(2)}) collective-permute-start(bf16[1,2,192,2048]{3,2,1,0:T(8,128)(2,1)S(1)} %copy-done.7), channel_id=1, source_target_pairs={{8,0},{16,8},{24,16},{0,24},{9,1},{17,9},{25,17},{1,25},{10,2},{18... | collective-permute-start | bytes 4718600 | tf_op jit(solution)/shard_map/ppermute | solution.py:27
  54.4 179.4 %collective-permute-start = (bf16[1,2,192,2048]{3,2,1,0:T(8,128)(2,1)}, bf16[1,2,192,2048]{3,2,1,0:T(8,128)(2,1)}, u32[]{:S(2)}, u32[]{:S(2)}) collective-permute-start(bf16[1,2,192,2048]{3,2,1,0:T(8,128)(2,1)} %param.5), channel_id=1, source_target_pairs={{24,0},{0,8},{8,16},{16,24},{25,1},{1,9},{9,17},{17,25},{26,2},{2,... | collective-permute-start | bytes 4718600 | tf_op jit(solution)/shard_map/ppermute | solution.py:27
  89.2 147.1 %copy-start.3 = (bf16[1,2,192,2048]{3,2,1,0:T(8,128)(2,1)}, bf16[1,2,192,2048]{3,2,1,0:T(8,128)(2,1)S(1)}, u32[]{:S(2)}) copy-start(bf16[1,2,192,2048]{3,2,1,0:T(8,128)(2,1)S(1)} %collective-permute-done.2) | copy-start | bytes 4718596
  232.3 21.4 %collective-permute-start.3 = (bf16[192,2048]{1,0:T(8,128)(2,1)S(1)}, bf16[192,2048]{1,0:T(8,128)(2,1)S(1)}, u32[]{:S(2)}, u32[]{:S(2)}) collective-permute-start(bf16[192,2048]{1,0:T(8,128)(2,1)S(1)} %get-tuple-element.12), channel_id=1, source_target_pairs={{0,2},{2,4},{4,6},{6,0},{1,3},{3,5},{5,7},{7,1},{8,10},{10,12},{12... | collective-permute-start | bytes 2359304 | tf_op jit(solution)/shard_map/ppermute | solution.py:12
  241.8 71.1 %all-to-all-start = ((bf16[192,4,1024]{2,0,1:T(8,128)(2,1)}), bf16[192,4,1024]{2,0,1:T(8,128)(2,1)}, u32[]{:S(2)}, u32[]{:S(2)}) async-start(bf16[192,4,1024]{2,0,1:T(8,128)(2,1)} %copy.10), calls=%async_computation.1 | async-start | bytes 3145728 | tf_op jit(solution)/shard_map/all_to_all | solution.py:72
  246.3 81.1 %reduce-scatter.2.cloned.1.call-start = ((), (), s32[]{:S(2)}) async-start(), calls=%async_computation.2 | async-start | bytes 2359296 | tf_op jit(solution)/shard_map/reduce_scatter | solution.py:67
  253.8 32.4 %collective-permute-start.4 = (bf16[192,2048]{1,0:T(8,128)(2,1)S(1)}, bf16[192,2048]{1,0:T(8,128)(2,1)S(1)}, u32[]{:S(2)}, u32[]{:S(2)}) collective-permute-start(bf16[192,2048]{1,0:T(8,128)(2,1)S(1)} %collective-permute-done.3), channel_id=1, source_target_pairs={{0,2},{2,4},{4,6},{6,0},{1,3},{3,5},{5,7},{7,1},{8,10},{10,12},{12... | collective-permute-start | bytes 2359304 | tf_op jit(solution)/shard_map/ppermute | solution.py:12
  286.1 19.2 %collective-permute-start.5 = (bf16[192,2048]{1,0:T(8,128)(2,1)S(1)}, bf16[192,2048]{1,0:T(8,128)(2,1)S(1)}, u32[]{:S(2)}, u32[]{:S(2)}) collective-permute-start(bf16[192,2048]{1,0:T(8,128)(2,1)S(1)} %collective-permute-done.4), channel_id=1, source_target_pairs={{0,2},{2,4},{4,6},{6,0},{1,3},{3,5},{5,7},{7,1},{8,10},{10,12},{12... | collective-permute-start | bytes 2359304 | tf_op jit(solution)/shard_map/ppermute | solution.py:12
  286.6 10.0 %copy-start.2 = (bf16[1,192,2048]{2,1,0:T(8,128)(2,1)S(1)}, bf16[1,192,2048]{2,1,0:T(8,128)(2,1)}, u32[]{:S(2)}) copy-start(bf16[1,192,2048]{2,1,0:T(8,128)(2,1)} %get-tuple-element.17) | copy-start | bytes 2359300
  296.6 1.3 copy-start.1
  296.7 1.9 copy-start.5
  320.8 6.5 %copy-start.4 = (bf16[1,2,192,2048]{3,2,1,0:T(8,128)(2,1)S(1)}, bf16[1,2,192,2048]{3,2,1,0:T(8,128)(2,1)}, u32[]{:S(2)}) copy-start(bf16[1,2,192,2048]{3,2,1,0:T(8,128)(2,1)} %copy-done.3) | copy-start | bytes 4718596
  327.4 1.5 copy-start
Sparse Core Ops, SparseCore 0:
  49.0 11.6 all-gather.10
  62.5 158.4 all-gather.8
  236.4 9.7 all-gather.6
  266.9 9.9 reduce-scatter.1
